TPU v7x, 32 devices: a whole 2x2x4 slice. The times are simulated.
32 devices in a mesh: seq: 2 (over x), fsdp: 16 (over z, y, core).
Axes of the slice: x: 2, y: 2, z: 4, core: 2. Of those that a mesh axis runs over, the one named last changes fastest.
Arguments:
- tokens: bfloat16 [4096, 1024], P(('fsdp', 'seq')), may hold values from -6 to 6
- cotangent: bfloat16 [4096, 1024], P(('fsdp', 'seq')), may hold values from -6 to 6
- documents: int32 [16, 256], P('fsdp'), may hold values from 0 to 3, never falling along the last dimension, each value on 1 to 128 neighbouring positions
- in_weight: bfloat16 [1024, 4384], P('fsdp'), may hold values from -0.1875 to 0.1875
- kernel_taps: float32 [4, 2304], replicated, may hold values from -3 to 3
- kernel_bias: float32 [2304], replicated, may hold values from -0.5 to 0.5
- step_bias: float32 [32], replicated, may hold values from -6 to -2
- decay_log: float32 [32], replicated, may hold values from 0 to 2.77
- skip_gain: float32 [32], replicated, may hold values from 0.5 to 1.5
- pre_gain: float32 [1024], replicated, may hold values from 0.5 to 1.5
- norm_gain: float32 [2048], replicated, may hold values from 0.5 to 1.5
- out_weight: bfloat16 [2048, 1024], P('fsdp'), may hold values from -0.125 to 0.125
Outputs:
- block_output: bfloat16 [4096, 1024], P(('fsdp', 'seq'))
- tokens_grad: float32 [4096, 1024], P(('fsdp', 'seq'))
- in_weight_grad: float32 [1024, 4384], P('fsdp')
- kernel_taps_grad: float32 [4, 2304], replicated
- kernel_bias_grad: float32 [2304], replicated
- step_bias_grad: float32 [32], replicated
- decay_log_grad: float32 [32], replicated
- skip_gain_grad: float32 [32], replicated
- pre_gain_grad: float32 [1024], replicated
- norm_gain_grad: float32 [2048], replicated
- out_weight_grad: float32 [2048, 1024], P('fsdp')
Inputs may be any that keep to these rules, and one draw needn't show every extreme that they name: `documents`: in every sequence the ids start at 0 and never fall; each id marks one document of consecutive tokens, and every id of 0 to 3 occurs.
All inputs are finite; a program needn't handle non-finite values.
Results may differ from a plain program's by a relative error of at most 0.011.
Values may be sent and summed in bfloat16 or wider, within the bound.
A program may use at most 128 MiB of HBM per device.

v0:
```python
from functools import partial
import jax
import jax.numpy as jnp
from jax import lax
from jax.sharding import PartitionSpec as P

HEADS = 32
HEAD_DIM = 64
STATE = 128
CONV = 4
SPAN = 256
INNER = 2048
CONV_CH = 2304
norm_epsilon = 1e-05


def pre_norm(values, gain):
    scale = lax.rsqrt(jnp.mean(values * values, axis=-1, keepdims=True) + norm_epsilon)
    return values * scale * gain


def gate_norm(mixed, gates, gain):
    gated = mixed * jax.nn.silu(gates)
    scale = lax.rsqrt(jnp.mean(gated * gated, axis=-1, keepdims=True) + norm_epsilon)
    return gated * scale * gain


def block_step(state, block):
    scaled, input_matrix, output_matrix, log_block, seg_block, prev_last = block
    width = seg_block.shape[0]
    cumul = jnp.cumsum(log_block, axis=0).T
    places = jnp.arange(width)
    causal = (places[:, None] >= places[None, :]) & (seg_block[:, None] == seg_block[None, :])
    log_gap = cumul[:, :, None] - cumul[:, None, :]
    decay = jnp.where(causal[None], jnp.exp(jnp.where(causal[None], log_gap, 0.0)), 0.0)
    scores = jnp.dot(output_matrix, input_matrix.T, precision=lax.Precision.HIGHEST)
    inside = jnp.einsum(
        "hij,jhp->ihp", decay * scores[None], scaled, precision=lax.Precision.HIGHEST
    )
    entering = jnp.exp(cumul) * (seg_block == prev_last).astype(jnp.float32)[None]
    carried = (
        jnp.einsum("in,hnp->ihp", output_matrix, state, precision=lax.Precision.HIGHEST)
        * entering.T[:, :, None]
    )
    final = cumul[:, -1]
    leaving = (
        jnp.exp(final[:, None] - cumul) * (seg_block == seg_block[-1]).astype(jnp.float32)[None]
    )
    fresh = jnp.einsum(
        "hj,jn,jhp->hnp", leaving, input_matrix, scaled, precision=lax.Precision.HIGHEST
    )
    keeping = jnp.exp(final) * (seg_block[-1] == prev_last).astype(jnp.float32)
    new_state = keeping[:, None, None] * state + fresh
    return (new_state, inside + carried)


def mixer(segment, conv_in, step_raw, taps, tap_bias, bias_steps, log_rates, skips):
    length, channels = conv_in.shape
    heads = step_raw.shape[1]
    width = heads * HEAD_DIM
    summed = tap_bias + conv_in * taps[CONV - 1]
    for offset in range(1, CONV):
        shifted = jnp.concatenate(
            [jnp.zeros((offset, channels), jnp.float32), conv_in[: length - offset]], axis=0
        )
        matched = jnp.concatenate(
            [
                jnp.zeros((offset,), jnp.float32),
                (segment[offset:] == segment[: length - offset]).astype(jnp.float32),
            ]
        )
        summed = summed + taps[CONV - 1 - offset] * shifted * matched[:, None]
    active = jax.nn.silu(summed)
    values = active[:, :width].reshape(length, heads, HEAD_DIM)
    input_matrix = active[:, width : width + STATE]
    output_matrix = active[:, width + STATE :]
    steps_taken = jax.nn.softplus(step_raw + bias_steps)
    log_decay = steps_taken * -jnp.exp(log_rates)
    scaled = values * steps_taken[:, :, None]
    blocks = length // SPAN
    seg_blocks = segment.reshape(blocks, SPAN)
    prev_last = jnp.concatenate([seg_blocks[:1, 0], seg_blocks[:-1, -1]])
    initial = jnp.zeros((heads, STATE, HEAD_DIM), jnp.float32)
    _, outputs = lax.scan(
        block_step,
        initial,
        (
            scaled.reshape(blocks, SPAN, heads, HEAD_DIM),
            input_matrix.reshape(blocks, SPAN, STATE),
            output_matrix.reshape(blocks, SPAN, STATE),
            log_decay.reshape(blocks, SPAN, heads),
            seg_blocks,
            prev_last,
        ),
    )
    result = outputs.reshape(length, heads, HEAD_DIM) + values * skips[None, :, None]
    return result.reshape(length, width)


def local(
    tokens,
    cotangent,
    documents,
    in_weight,
    kernel_taps,
    kernel_bias,
    step_bias,
    decay_log,
    skip_gain,
    pre_gain,
    norm_gain,
    out_weight,
):
    group_count = lax.axis_size("seq")
    group_index = lax.axis_index("seq")
    local_heads = HEADS // group_count
    local_width = local_heads * HEAD_DIM
    head_start = group_index * local_width
    head_first = group_index * local_heads
    contract_rows = (((1,), (1,)), ((), ()))
    contract_tokens = (((0,), (0,)), ((), ()))
    floats = tokens.astype(jnp.float32)
    normed_in = pre_norm(floats, pre_gain).astype(jnp.bfloat16)
    in_whole = lax.all_gather(in_weight, "fsdp", axis=0, tiled=True)
    projected = jnp.dot(normed_in, in_whole, preferred_element_type=jnp.float32).astype(
        jnp.bfloat16
    )
    gates = projected[:, :INNER]
    values_raw = projected[:, INNER : 2 * INNER]
    state_raw = projected[:, 2 * INNER : INNER + CONV_CH]
    step_raw = projected[:, INNER + CONV_CH :]
    head_values, head_steps = (
        lax.all_to_all(values_raw, "seq", split_axis=1, concat_axis=0, tiled=True),
        lax.all_to_all(step_raw, "seq", split_axis=1, concat_axis=0, tiled=True),
    )
    state_whole = lax.all_gather(state_raw, "seq", axis=0, tiled=True)
    segment = documents[0]
    local_taps = jnp.concatenate(
        [lax.dynamic_slice_in_dim(kernel_taps, head_start, local_width, 1), kernel_taps[:, INNER:]],
        axis=1,
    )
    local_bias = jnp.concatenate(
        [lax.dynamic_slice_in_dim(kernel_bias, head_start, local_width, 0), kernel_bias[INNER:]],
        axis=0,
    )
    local_step_bias = lax.dynamic_slice_in_dim(step_bias, head_first, local_heads, 0)
    local_decay = lax.dynamic_slice_in_dim(decay_log, head_first, local_heads, 0)
    local_skip = lax.dynamic_slice_in_dim(skip_gain, head_first, local_heads, 0)
    conv_in = jnp.concatenate(
        [head_values.astype(jnp.float32), state_whole.astype(jnp.float32)], axis=1
    )
    mixed, mixer_back = jax.vjp(
        partial(mixer, segment),
        conv_in,
        head_steps.astype(jnp.float32),
        local_taps,
        local_bias,
        local_step_bias,
        local_decay,
        local_skip,
    )
    token_mixed = lax.all_to_all(
        mixed.astype(jnp.bfloat16), "seq", split_axis=0, concat_axis=1, tiled=True
    )
    normed_out, norm_back = jax.vjp(
        gate_norm, token_mixed.astype(jnp.float32), gates.astype(jnp.float32), norm_gain
    )
    normed_bf = normed_out.astype(jnp.bfloat16)
    out_whole = lax.all_gather(out_weight, "fsdp", axis=0, tiled=True)
    branch = jnp.dot(normed_bf, out_whole, preferred_element_type=jnp.float32)
    block_output = (floats + branch).astype(jnp.bfloat16)
    back_normed = lax.dot_general(
        cotangent, out_whole, contract_rows, preferred_element_type=jnp.float32
    )
    columns = normed_bf
    outward_grad = lax.psum_scatter(
        lax.dot_general(columns, cotangent, contract_tokens, preferred_element_type=jnp.float32),
        "fsdp",
        scatter_dimension=0,
        tiled=True,
    )
    back_mixed, back_gates, norm_gain_part = norm_back(back_normed)
    head_back = lax.all_to_all(
        back_mixed.astype(jnp.bfloat16), "seq", split_axis=1, concat_axis=0, tiled=True
    )
    back_conv, back_steps, taps_part, bias_part, step_part, decay_part, skip_part = mixer_back(
        head_back.astype(jnp.float32)
    )
    back_values, back_step_tokens = (
        lax.all_to_all(
            back_conv[:, :local_width].astype(jnp.bfloat16),
            "seq",
            split_axis=0,
            concat_axis=1,
            tiled=True,
        ),
        lax.all_to_all(
            back_steps.astype(jnp.bfloat16), "seq", split_axis=0, concat_axis=1, tiled=True
        ),
    )
    back_state = lax.psum_scatter(
        back_conv[:, local_width:].astype(jnp.bfloat16), "seq", scatter_dimension=0, tiled=True
    )
    back_projected = jnp.concatenate(
        [back_gates.astype(jnp.bfloat16), back_values, back_state, back_step_tokens], axis=1
    )
    back_normed_in = lax.dot_general(
        back_projected, in_whole, contract_rows, preferred_element_type=jnp.float32
    )
    columns = normed_in
    inward_grad = lax.psum_scatter(
        lax.dot_general(
            columns, back_projected, contract_tokens, preferred_element_type=jnp.float32
        ),
        "fsdp",
        scatter_dimension=0,
        tiled=True,
    )
    inward_grad, outward_grad = lax.psum((inward_grad, outward_grad), "seq")
    _, pre_back = jax.vjp(pre_norm, floats, pre_gain)
    back_floats, pre_gain_part = pre_back(back_normed_in)
    tokens_grad = cotangent.astype(jnp.float32) + back_floats
    taps_full = lax.dynamic_update_slice_in_dim(
        jnp.zeros_like(kernel_taps), taps_part[:, :local_width], head_start, 1
    )
    taps_full = taps_full.at[:, INNER:].set(taps_part[:, local_width:])
    bias_full = lax.dynamic_update_slice_in_dim(
        jnp.zeros_like(kernel_bias), bias_part[:local_width], head_start, 0
    )
    bias_full = bias_full.at[INNER:].set(bias_part[local_width:])
    step_full = lax.dynamic_update_slice_in_dim(jnp.zeros_like(step_bias), step_part, head_first, 0)
    decay_full = lax.dynamic_update_slice_in_dim(
        jnp.zeros_like(decay_log), decay_part, head_first, 0
    )
    skip_full = lax.dynamic_update_slice_in_dim(jnp.zeros_like(skip_gain), skip_part, head_first, 0)
    totals = lax.psum(
        (taps_full, bias_full, step_full, decay_full, skip_full, pre_gain_part, norm_gain_part),
        ("seq", "fsdp"),
    )
    return (
        block_output,
        tokens_grad,
        inward_grad,
        totals[0],
        totals[1],
        totals[2],
        totals[3],
        totals[4],
        totals[5],
        totals[6],
        outward_grad,
    )


def solution(mesh):
    return jax.shard_map(
        local,
        mesh=mesh,
        in_specs=(
            P(("fsdp", "seq"), None),
            P(("fsdp", "seq"), None),
            P("fsdp", None),
            P("fsdp", None),
            P(),
            P(),
            P(),
            P(),
            P(),
            P(),
            P(),
            P("fsdp", None),
        ),
        out_specs=(
            P(("fsdp", "seq"), None),
            P(("fsdp", "seq"), None),
            P("fsdp", None),
            P(),
            P(),
            P(),
            P(),
            P(),
            P(),
            P(),
            P("fsdp", None),
        ),
        check_vma=False,
    )
```

profile of v0, /device:TPU:0, one launch (start us, length us, event | category | flops | bytes accessed | tf_op | source)
XLA Modules:
  0.0 587.1 jit_solution(15330456754907170330)
XLA Ops:
  20.2 2.6 compare_convert_fusion
  22.7 1.5 fusion.67
  24.2 68.1 %all-gather.3.cloned.1.call-done = bf16[1024,4384]{1,0:T(8,128)(2,1)} async-done(((bf16[64,4384]{1,0:T(8,128)(2,1)}), bf16[1024,4384]{1,0:T(8,128)(2,1)}) %all-gather.3.cloned.1.call-update) | async-done | bytes 8978448 | tf_op jit(solution)/shard_map/all_gather | solution.py:124
  92.3 7.3 %convolution_convert_fusion = bf16[128,4384]{0,1:T(8,128)(2,1)S(1)} fusion(bf16[1024,4384]{1,0:T(8,128)(2,1)} %all-gather.3.cloned.1.call-done, bf16[128,1024]{1,0:T(8,128)(2,1)S(1)} %copy-done.4, f32[1024]{0:T(1024)S(1)} %copy-done.23, f32[128]{0:T(128)S(1)} %fusion.99), kind=kOutput, calls=%fused_computation | convolution fusion | flops 1150324736 | bytes 10367488 | tf_op jit(solution)/shard_map/dot_general | solution.py:125
  100.3 3.2 all-to-all-start
  103.6 5.0 all_gather.10
  109.5 3.8 all-to-all-start.1
  115.6 5.5 all-to-all-done.1
  121.6 2.1 fusion.32
  125.3 2.9 multiply_reduce_fusion.5
  129.6 1.4 fusion.73
  130.9 2.0 fusion.61
  133.0 6.2 %fusion.27 = f32[256,16,64]{0,2,1:T(8,128)} fusion(f32[256,256]{1,0:T(8,128)S(1)} %fusion.73, f32[16,256]{1,0:T(8,128)S(1)} %copy-done.44, pred[256,256]{1,0:T(8,128)(4,1)S(1)} %copy-done.47, f32[256,16,64]{0,2,1:T(8,128)S(1)} %bitcast.205, f32[256,16,64]{0,2,1:T(8,128)S(1)} %bitcast.193, f32[256,16]{0,1:T(8,128)S(1)} %get-tuple-element.355, ...), kind=kOutput, calls=%fused_computation.29 | convolution fusion | flops 810287104 | bytes 3522560 | tf_op jit(solution)/shard_map/jvp()/while/body/eval_jaxpr/hij,jhp->ihp/dot_general | solution.py:37
  139.2 1.6 copy.126
  140.7 2.2 add_convert_fusion.1
  144.3 9.4 %all_to_all.93 = bf16[2,128,1024]{1,2,0:T(8,128)(2,1)S(1)} all-to-all(bf16[2,128,1024]{1,2,0:T(8,128)(2,1)S(1)} %copy.127), channel_id=1, replica_groups=mesh['seq'=2,'fsdp'=16] {'seq'}, dimensions={0} | all-to-all | bytes 1048576 | tf_op jit(solution)/shard_map/all_to_all | solution.py:162
  154.4 1.4 multiply_reduce_fusion.9
  156.9 4.2 multiply_reduce_fusion.6
  161.2 2.8 fusion.41
  164.0 4.2 all-to-all-start.3
  168.8 1.8 mul.622
  170.6 2.7 mul.647
  173.3 3.2 convolution_bitcast_fusion
  176.5 2.4 copy.131
  178.8 2.2 squeeze.106
  181.1 5.8 fusion.7
  186.9 4.8 fusion.34
  191.7 2.7 copy.132
  196.3 1.8 mul.649
  198.1 3.2 convolution_bitcast_fusion.1
  201.3 1.6 convolution_add_fusion.1
  203.0 1.4 convolution_add_fusion.2
  210.0 4.6 fusion.110
  215.6 2.5 reduce-window.28
  219.0 3.2 all-to-all-start.5
  223.4 2.7 all-to-all-done.5
  226.1 3.5 all-to-all-start.4
  230.6 5.5 all-to-all-done.4
  236.2 9.2 %fusion.68 = f32[1024,4384]{1,0:T(8,128)} fusion(bf16[128,32]{0,1:T(8,128)(2,1)S(1)} %bitcast.211, bf16[128,256]{0,1:T(8,128)(2,1)S(1)} %copy.149, bf16[128,2048]{0,1:T(8,128)(2,1)S(1)} %bitcast.199, bf16[128,2048]{0,1:T(8,128)(2,1)S(1)} %copy-done.13, bf16[128,1024]{1,0:T(8,128)(2,1)S(1)} %copy-done.5, f32[1024]{0:T(1024)S(1)} %copy-done.24, ...), kind=kOutput, calls=%fused_computation.108 | convolution fusion | flops 1154252800 | bytes 19345920 | tf_op jit(solution)/shard_map/dot_general | solution.py:212
  245.5 4.2 fusion.33
  249.8 2.1 bitcast_convert_fusion
  251.9 1.7 copy.139
  253.8 73.3 %reduce-scatter.8.cloned.1.call-done = f32[128,1024]{1,0:T(8,128)} async-done(((f32[2048,1024]{1,0:T(8,128)}), f32[128,1024]{1,0:T(8,128)}) %reduce-scatter.8.cloned.1.call-update) | async-done | bytes 524304 | tf_op jit(solution)/shard_map/reduce_scatter | solution.py:176
  327.0 193.4 %reduce-scatter.6.cloned.1.call-done = f32[64,4384]{1,0:T(8,128)} async-done(((f32[1024,4384]{1,0:T(8,128)}), f32[64,4384]{1,0:T(8,128)}) %reduce-scatter.6.cloned.1.call-update) | async-done | bytes 1122320 | tf_op jit(solution)/shard_map/reduce_scatter | solution.py:211
  521.7 6.8 %fusion.51 = (f32[1024]{0:T(1024)S(1)}, f32[128]{0:T(128)S(1)}, f32[128,1024]{1,0:T(8,128)S(1)}) fusion(bf16[128,1024]{1,0:T(8,128)(2,1)S(1)} %copy-done.5, f32[128]{0:T(128)S(1)} %copy-done.59, f32[1024]{0:T(1024)S(1)} %copy-done.24, bf16[1024,4384]{1,0:T(8,128)(2,1)} %all-gather.3.cloned.1.call-done, bf16[128,32]{0,1:T(8,128)(2,1)S(1)} %bitcast.212, ...), kind=kOutput, calls=%fused_computation.90 | convolution fusion | flops 1154644864 | bytes 10896384 | tf_op jit(solution)/shard_map/dot_general | solution.py:207
  528.5 41.8 %all-reduce.16 = (f32[4,2304]{1,0:T(4,128)}, f32[2304]{0:T(1024)}, f32[32]{0:T(128)}, f32[32]{0:T(128)}, f32[32]{0:T(128)}, /*index=5*/f32[1024]{0:T(1024)}, f32[2048]{0:T(1024)}) all-reduce(f32[4,2304]{1,0:T(4,128)S(1)} %add_dynamic-update-slice_fusion, ...), channel_id=1, replica_groups=mesh['seq'=2,'fsdp'=16] {'seq','fsdp'}, use_global_device_ids=true, to_apply=%region_21.22 | all-reduce | flops 14688 | bytes 117504 | tf_op jit(solution)/shard_map/psum | solution.py:236
  571.3 5.5 all-reduce.20.cloned.1.call-done
  576.8 2.4 copy.200
  (272 shorter events, 38.3 us)
Async XLA Ops:
  7.2 85.1 %copy-start.4 = (bf16[128,1024]{1,0:T(8,128)(2,1)S(1)}, bf16[128,1024]{1,0:T(8,128)(2,1)}, u32[]{:S(2)}) copy-start(bf16[128,1024]{1,0:T(8,128)(2,1)} %param.16) | copy-start | bytes 786436
  7.2 85.1 %copy-start.23 = (f32[1024]{0:T(1024)S(1)}, f32[1024]{0:T(1024)}, u32[]{:S(2)}) copy-start(f32[1024]{0:T(1024)} %param.25) | copy-start | bytes 12292
  7.2 85.1 %all-gather.3.cloned.1.call-start = ((), (), s32[]{:S(2)}) async-start(), calls=%async_computation.9 | async-start | bytes 9748480 | tf_op jit(solution)/shard_map/all_gather | solution.py:124
  7.9 148.9 %all-gather.5.cloned.1.call-start = ((), (), s32[]{:S(2)}) async-start(), calls=%async_computation.10 | async-start | bytes 4456448 | tf_op jit(solution)/shard_map/all_gather | solution.py:169
  11.6 101.8 %copy-start.74 = (f32[16]{0:T(128)}, f32[16]{0:T(128)S(1)}, u32[]{:S(2)}) copy-start(f32[16]{0:T(128)S(1)} %dynamic_slice.89) | copy-start | bytes 196
  14.3 107.2 %copy-start.31 = (f32[1280]{0:T(1024)}, f32[1280]{0:T(1024)S(1)}, u32[]{:S(2)}) copy-start(f32[1280]{0:T(1024)S(1)} %get-tuple-element.316) | copy-start | bytes 15364
  14.3 107.2 %copy-start.33 = (f32[1280]{0:T(1024)}, f32[1280]{0:T(1024)S(1)}, u32[]{:S(2)}) copy-start(f32[1280]{0:T(1024)S(1)} %get-tuple-element.318) | copy-start | bytes 15364
  14.3 107.2 %copy-start.35 = (f32[1280]{0:T(1024)}, f32[1280]{0:T(1024)S(1)}, u32[]{:S(2)}) copy-start(f32[1280]{0:T(1024)S(1)} %get-tuple-element.319) | copy-start | bytes 15364
  14.3 107.2 %copy-start.37 = (f32[1280]{0:T(1024)}, f32[1280]{0:T(1024)S(1)}, u32[]{:S(2)}) copy-start(f32[1280]{0:T(1024)S(1)} %get-tuple-element.317) | copy-start | bytes 15364
  15.1 98.3 %copy-start.76 = (f32[16]{0:T(128)}, f32[16]{0:T(128)S(1)}, u32[]{:S(2)}) copy-start(f32[16]{0:T(128)S(1)} %fusion.100) | copy-start | bytes 196
  16.0 105.5 %copy-start.72 = (f32[256]{0:T(256)}, f32[256]{0:T(256)S(1)}, u32[]{:S(2)}) copy-start(f32[256]{0:T(256)S(1)} %pad_convert_fusion.1) | copy-start | bytes 3076
  17.8 103.8 %copy-start.66 = (f32[256]{0:T(256)}, f32[256]{0:T(256)S(1)}, u32[]{:S(2)}) copy-start(f32[256]{0:T(256)S(1)} %get-tuple-element.364) | copy-start | bytes 3076
  17.8 103.8 %copy-start.68 = (f32[256]{0:T(256)}, f32[256]{0:T(256)S(1)}, u32[]{:S(2)}) copy-start(f32[256]{0:T(256)S(1)} %get-tuple-element.365) | copy-start | bytes 3076
  20.2 79.5 %copy-start.79 = (f32[128]{0:T(128)}, f32[128]{0:T(128)S(1)}, u32[]{:S(2)}) copy-start(f32[128]{0:T(128)S(1)} %fusion.53) | copy-start | bytes 1540
  20.2 79.4 %copy-start.58 = (f32[128]{0:T(128)}, f32[128]{0:T(128)S(1)}, u32[]{:S(2)}) copy-start(f32[128]{0:T(128)S(1)} %fusion.99) | copy-start | bytes 1540
  99.6 9.9 %copy-start.6 = (bf16[128,4384]{0,1:T(8,128)(2,1)}, bf16[128,4384]{0,1:T(8,128)(2,1)S(1)}, u32[]{:S(2)}) copy-start(bf16[128,4384]{0,1:T(8,128)(2,1)S(1)} %convolution_convert_fusion) | copy-start | bytes 3366916
  100.3 9.2 %all-to-all-start = ((bf16[128,2,16]{0,2,1:T(8,128)(2,1)}), bf16[128,2,16]{0,2,1:T(8,128)(2,1)S(1)}, u32[]{:S(2)}, u32[]{:S(2)}) async-start(bf16[128,2,16]{0,2,1:T(8,128)(2,1)} %bitcast.3), calls=%async_computation | async-start | bytes 16384 | tf_op jit(solution)/shard_map/all_to_all | solution.py:134
  109.5 11.6 %copy-start.39 = (bf16[128,2,16]{0,2,1:T(8,128)(2,1)}, bf16[128,2,16]{0,2,1:T(8,128)(2,1)S(1)}, u32[]{:S(2)}) copy-start(bf16[128,2,16]{0,2,1:T(8,128)(2,1)S(1)} %all-to-all-done) | copy-start | bytes 24580
  109.5 11.6 %all-to-all-start.1 = ((bf16[128,2,1024]{0,2,1:T(8,128)(2,1)}), bf16[128,2,1024]{0,2,1:T(8,128)(2,1)S(1)}, u32[]{:S(2)}, u32[]{:S(2)}) async-start(bf16[128,2,1024]{0,2,1:T(8,128)(2,1)} %bitcast.6), calls=%async_computation.1 | async-start | bytes 1048576 | tf_op jit(solution)/shard_map/all_to_all | solution.py:133
  114.8 6.6 %copy-start.51 = (f32[16,2]{0,1:T(2,128)}, f32[16,2]{0,1:T(2,128)S(1)}, u32[]{:S(2)}) copy-start(f32[16,2]{0,1:T(2,128)S(1)} %slice.164) | copy-start | bytes 388
  114.9 6.5 %copy-start.43 = (f32[16,256]{1,0:T(8,128)}, f32[16,256]{1,0:T(8,128)S(1)}, u32[]{:S(2)}) copy-start(f32[16,256]{1,0:T(8,128)S(1)} %copy_bitcast_fusion) | copy-start | bytes 49156
  129.6 9.6 %copy-start.42 = (f32[256,16]{0,1:T(8,128)}, f32[256,16]{0,1:T(8,128)S(1)}, u32[]{:S(2)}) copy-start(f32[256,16]{0,1:T(8,128)S(1)} %get-tuple-element.355) | copy-start | bytes 49156
  130.9 8.3 %copy-start.25 = (f32[256,256]{1,0:T(8,128)}, f32[256,256]{1,0:T(8,128)S(1)}, u32[]{:S(2)}) copy-start(f32[256,256]{1,0:T(8,128)S(1)} %fusion.73) | copy-start | bytes 786436
  132.9 6.2 %copy-start.16 = (f32[256,1024]{0,1}, f32[256,1024]{0,1:S(1)}, u32[]{:S(2)}) copy-start(f32[256,1024]{0,1:S(1)} %fusion.61) | copy-start | bytes 3145732
  164.0 12.5 %all-to-all-start.3 = ((bf16[128,2,1024]{0,2,1:T(8,128)(2,1)}), bf16[128,2,1024]{0,2,1:T(8,128)(2,1)}, u32[]{:S(2)}, u32[]{:S(2)}) async-start(bf16[128,2,1024]{0,2,1:T(8,128)(2,1)} %bitcast.201), calls=%async_computation.3 | async-start | bytes 1048576 | tf_op jit(solution)/shard_map/all_to_all | solution.py:183
  168.2 61.5 %reduce-scatter.10.cloned.1.call-start = ((), (), s32[]{:S(2)}) async-start(), calls=%async_computation.13 | async-start | bytes 196608
  181.0 5.8 copy-start.18
  181.0 5.8 copy-start.20
  181.0 5.8 copy-start.26
  181.0 5.8 copy-start.28
  198.1 6.2 %copy-start.7 = (f32[256,1280]{1,0:T(8,128)S(1)}, f32[256,1280]{1,0:T(8,128)}, u32[]{:S(2)}) copy-start(f32[256,1280]{1,0:T(8,128)} %get-tuple-element.341) | copy-start | bytes 3932164
  198.1 6.2 %copy-start.11 = (f32[256,1024]{1,0:T(8,128)S(1)}, f32[256,1024]{1,0:T(8,128)}, u32[]{:S(2)}) copy-start(f32[256,1024]{1,0:T(8,128)} %copy.132) | copy-start | bytes 3145732
  198.1 6.2 %copy-start.69 = (f32[256]{0:T(256)S(1)}, f32[256]{0:T(256)}, u32[]{:S(2)}) copy-start(f32[256]{0:T(256)} %copy-done.68) | copy-start | bytes 3076
  209.9 117.1 %reduce-scatter.8.cloned.1.call-start = ((), (), s32[]{:S(2)}) async-start(), calls=%async_computation.12 | async-start | bytes 8912896 | tf_op jit(solution)/shard_map/reduce_scatter | solution.py:176
  219.0 7.0 %all-to-all-start.5 = ((bf16[2,128,16]{1,2,0:T(8,128)(2,1)}), bf16[2,128,16]{1,2,0:T(8,128)(2,1)S(1)}, u32[]{:S(2)}, u32[]{:S(2)}) async-start(bf16[2,128,16]{1,2,0:T(8,128)(2,1)} %copy_bitcast_fusion.3), calls=%async_computation.5 | async-start | bytes 16384 | tf_op jit(solution)/shard_map/all_to_all | solution.py:197
  222.3 13.8 %copy-start.5 = (bf16[128,1024]{1,0:T(8,128)(2,1)S(1)}, bf16[128,1024]{1,0:T(8,128)(2,1)}, u32[]{:S(2)}) copy-start(bf16[128,1024]{1,0:T(8,128)(2,1)} %param.16) | copy-start | bytes 786436
  222.3 13.8 %copy-start.13 = (bf16[128,2048]{0,1:T(8,128)(2,1)S(1)}, bf16[128,2048]{0,1:T(8,128)(2,1)}, u32[]{:S(2)}) copy-start(bf16[128,2048]{0,1:T(8,128)(2,1)} %get-tuple-element.342) | copy-start | bytes 1572868
  222.4 13.8 %copy-start.24 = (f32[1024]{0:T(1024)S(1)}, f32[1024]{0:T(1024)}, u32[]{:S(2)}) copy-start(f32[1024]{0:T(1024)} %param.25) | copy-start | bytes 12292
  222.4 13.8 %copy-start.59 = (f32[128]{0:T(128)S(1)}, f32[128]{0:T(128)}, u32[]{:S(2)}) copy-start(f32[128]{0:T(128)} %copy-done.58) | copy-start | bytes 1540
  226.1 10.1 %all-to-all-start.4 = ((bf16[2,128,1024]{1,2,0:T(8,128)(2,1)}), bf16[2,128,1024]{1,2,0:T(8,128)(2,1)S(1)}, u32[]{:S(2)}, u32[]{:S(2)}) async-start(bf16[2,128,1024]{1,2,0:T(8,128)(2,1)} %copy.133), calls=%async_computation.4 | async-start | bytes 1048576 | tf_op jit(solution)/shard_map/all_to_all | solution.py:190
  229.6 290.9 %reduce-scatter.6.cloned.1.call-start = ((), (), s32[]{:S(2)}) async-start(), calls=%async_computation.11 | async-start | bytes 19496960 | tf_op jit(solution)/shard_map/reduce_scatter | solution.py:211
  236.2 9.3 %copy-start.14 = (bf16[2,128,1024]{1,2,0:T(8,128)(2,1)}, bf16[2,128,1024]{1,2,0:T(8,128)(2,1)S(1)}, u32[]{:S(2)}) copy-start(bf16[2,128,1024]{1,2,0:T(8,128)(2,1)S(1)} %all-to-all-done.4) | copy-start | bytes 1572868
  245.5 331.4 %all-reduce.20.cloned.1.call-start = ((), (), s32[]{:S(2)}) async-start(), calls=%async_computation.14 | async-start | bytes 3342336 | tf_op jit(solution)/shard_map/psum | solution.py:219
  253.7 266.8 %copy-start.49 = (f32[1280]{0:T(1024)S(1)}, f32[1280]{0:T(1024)}, u32[]{:S(2)}) copy-start(f32[1280]{0:T(1024)} %get-tuple-element.312) | copy-start | bytes 15364
  253.7 267.8 %copy-start.85 = (f32[32]{0:T(128)S(1)}, f32[32]{0:T(128)}, u32[]{:S(2)}) copy-start(f32[32]{0:T(128)} %param.23) | copy-start | bytes 388
  253.7 267.9 %copy-start.15 = (bf16[2,128,1024]{1,2,0:T(8,128)(2,1)S(1)}, bf16[2,128,1024]{1,2,0:T(8,128)(2,1)}, u32[]{:S(2)}) copy-start(bf16[2,128,1024]{1,2,0:T(8,128)(2,1)} %copy-done.14) | copy-start | bytes 1572868
  521.6 6.8 %copy-start.50 = (f32[2048]{0:T(1024)S(1)}, f32[2048]{0:T(1024)}, u32[]{:S(2)}) copy-start(f32[2048]{0:T(1024)} %get-tuple-element.310) | copy-start | bytes 24580
  521.6 48.7 %copy-start.80 = (f32[128]{0:T(128)S(1)}, f32[128]{0:T(128)}, u32[]{:S(2)}) copy-start(f32[128]{0:T(128)} %copy-done.79) | copy-start | bytes 1540
  (49 other events, 118.7 us)
Sparse Core Ops, SparseCore 0:
  10.3 81.9 all-gather.2
  94.5 48.8 all-gather.4
  210.0 9.5 reduce-scatter.9
  223.5 103.4 reduce-scatter.7
  331.1 189.3 reduce-scatter.5
  522.7 54.1 all-reduce.19
where the time goes:
time: 593 us; the launch traced here: 587 us
  waiting for transfers between devices  356 us (60%)
  matrix products  68.8 us (12%)
  blocking collectives  56.2 us (9%)
  local copies, waits for them, and re-layouts  41.7 us (7%)
  other arithmetic  30.7 us (5%)
  starting transfers between devices  18.7 us (3%)
  between operations  15.5 us (3%)
    reduce_scatter x1, waiting for transfers between devices, local(): lax.psum_scatter(lax.dot_general(columns, back_projected, contract_tokens...  193 us
    reduce_scatter x1, waiting for transfers between devices, local(): lax.psum_scatter(lax.dot_general(columns, cotangent, contract_tokens, pre...  73.3 us
    all_gather x1, waiting for transfers between devices, local(): in_whole = lax.all_gather(in_weight, 'fsdp', axis=0, tiled=True)  68.1 us
    psum x1, blocking collectives, local(): lax.psum((taps_full, bias_full, step_full, decay_full, skip_full, pre_gai...  41.8 us
    dot_general x3, matrix products, block_step(): jnp.einsum('hij,jhp->ihp', decay * scores[None], scaled, precision=lax.Pr...  16.8 us
  transfers between devices with their start and end apart: 11, of which 7 were waited for; matrix products, arithmetic and copies ran while one was open for 16% of the time, Pallas kernels for 0%

commit v1 on v0

--- a/solution.py
+++ b/solution.py
@@ -233,10 +233,9 @@
         jnp.zeros_like(decay_log), decay_part, head_first, 0
     )
     skip_full = lax.dynamic_update_slice_in_dim(jnp.zeros_like(skip_gain), skip_part, head_first, 0)
-    totals = lax.psum(
-        (taps_full, bias_full, step_full, decay_full, skip_full, pre_gain_part, norm_gain_part),
-        ("seq", "fsdp"),
-    )
+    totals = (taps_full, bias_full, step_full, decay_full, skip_full, pre_gain_part, norm_gain_part)
+    for mesh_axis in ("fsdp", "seq"):
+        totals = lax.psum(totals, mesh_axis)
     return (
         block_output,
         tokens_grad,

time: 593 us -> 615 us (1.037)
  blocking collectives: 56.2 us -> 83.4 us
  waiting for transfers between devices: 356 us -> 349 us
    psum x1 -> x2, blocking collectives: 41.8 us -> 69 us  [local(): totals = lax.psum(totals, mesh_axis)]
  transfers between devices with their start and end apart: 11 -> 11, of which waited for: 7 -> 6; matrix products, arithmetic and copies ran while one was open for 16% -> 16% of each run, Pallas kernels for 0% -> 0%
where the time goes in v1:
time: 615 us; the launch traced here: 609 us
  waiting for transfers between devices  349 us (57%)
  blocking collectives  83.4 us (14%)
  matrix products  68.7 us (11%)
  local copies, waits for them, and re-layouts  42.8 us (7%)
  other arithmetic  31.4 us (5%)
  starting transfers between devices  18.7 us (3%)
  between operations  15.5 us (3%)
    reduce_scatter x1, waiting for transfers between devices, local(): lax.psum_scatter(lax.dot_general(columns, back_projected, contract_tokens...  193 us
    reduce_scatter x1, waiting for transfers between devices, local(): lax.psum_scatter(lax.dot_general(columns, cotangent, contract_tokens, pre...  71.8 us
    psum x2, blocking collectives, local(): totals = lax.psum(totals, mesh_axis)  69 us
    all_gather x1, waiting for transfers between devices, local(): in_whole = lax.all_gather(in_weight, 'fsdp', axis=0, tiled=True)  68.1 us
    dot_general x3, matrix products, block_step(): jnp.einsum('hij,jhp->ihp', decay * scores[None], scaled, precision=lax.Pr...  16.7 us
  transfers between devices with their start and end apart: 11, of which 6 were waited for; matrix products, arithmetic and copies ran while one was open for 16% of the time, Pallas kernels for 0%

profile of v1, /device:TPU:0, one launch (start us, length us, event | category | flops | bytes accessed | tf_op | source)
XLA Modules:
  0.0 609.0 jit_solution(440748634658551265)
XLA Ops:
  20.2 2.6 compare_convert_fusion
  22.8 1.5 fusion.67
  24.2 68.1 %all-gather.3.cloned.1.call-done = bf16[1024,4384]{1,0:T(8,128)(2,1)} async-done(((bf16[64,4384]{1,0:T(8,128)(2,1)}), bf16[1024,4384]{1,0:T(8,128)(2,1)}) %all-gather.3.cloned.1.call-update) | async-done | bytes 8978448 | tf_op jit(solution)/shard_map/all_gather | solution.py:124
  92.3 7.3 %convolution_convert_fusion = bf16[128,4384]{0,1:T(8,128)(2,1)S(1)} fusion(bf16[1024,4384]{1,0:T(8,128)(2,1)} %all-gather.3.cloned.1.call-done, bf16[128,1024]{1,0:T(8,128)(2,1)S(1)} %copy-done.4, f32[1024]{0:T(1024)S(1)} %copy-done.23, f32[128]{0:T(128)S(1)} %fusion.99), kind=kOutput, calls=%fused_computation | convolution fusion | flops 1150324736 | bytes 10367488 | tf_op jit(solution)/shard_map/dot_general | solution.py:125
  100.3 3.2 all-to-all-start
  103.6 5.0 all_gather.10
  109.5 3.8 all-to-all-start.1
  115.6 5.5 all-to-all-done.1
  121.6 2.1 fusion.32
  125.3 2.9 multiply_reduce_fusion.5
  129.6 1.4 fusion.73
  130.9 2.0 fusion.61
  133.0 6.2 %fusion.27 = f32[256,16,64]{0,2,1:T(8,128)} fusion(f32[256,256]{1,0:T(8,128)S(1)} %fusion.73, f32[16,256]{1,0:T(8,128)S(1)} %copy-done.44, pred[256,256]{1,0:T(8,128)(4,1)S(1)} %copy-done.47, f32[256,16,64]{0,2,1:T(8,128)S(1)} %bitcast.205, f32[256,16,64]{0,2,1:T(8,128)S(1)} %bitcast.193, f32[256,16]{0,1:T(8,128)S(1)} %get-tuple-element.362, ...), kind=kOutput, calls=%fused_computation.29 | convolution fusion | flops 810287104 | bytes 3522560 | tf_op jit(solution)/shard_map/jvp()/while/body/eval_jaxpr/hij,jhp->ihp/dot_general | solution.py:37
  139.2 1.6 copy.126
  140.7 2.2 add_convert_fusion.1
  144.3 9.4 %all_to_all.93 = bf16[2,128,1024]{1,2,0:T(8,128)(2,1)S(1)} all-to-all(bf16[2,128,1024]{1,2,0:T(8,128)(2,1)S(1)} %copy.127), channel_id=1, replica_groups=mesh['seq'=2,'fsdp'=16] {'seq'}, dimensions={0} | all-to-all | bytes 1048576 | tf_op jit(solution)/shard_map/all_to_all | solution.py:162
  154.4 1.4 multiply_reduce_fusion.9
  156.9 4.2 multiply_reduce_fusion.6
  161.2 2.8 fusion.41
  164.0 4.2 all-to-all-start.3
  168.8 1.8 mul.622
  170.5 2.7 mul.647
  173.3 3.2 convolution_bitcast_fusion
  176.5 2.4 copy.131
  178.8 2.2 squeeze.106
  181.1 5.8 fusion.7
  186.9 4.8 fusion.34
  191.7 2.7 copy.132
  196.3 1.8 mul.649
  198.1 3.2 convolution_bitcast_fusion.1
  201.3 1.6 convolution_add_fusion.1
  203.0 1.4 convolution_add_fusion.2
  210.5 4.6 fusion.110
  216.0 2.5 reduce-window.28
  219.5 3.2 all-to-all-start.5
  223.9 2.7 all-to-all-done.5
  226.6 3.5 all-to-all-start.4
  231.1 5.5 all-to-all-done.4
  236.7 9.2 %fusion.68 = f32[1024,4384]{1,0:T(8,128)} fusion(bf16[128,32]{0,1:T(8,128)(2,1)S(1)} %bitcast.211, bf16[128,256]{0,1:T(8,128)(2,1)S(1)} %copy.149, bf16[128,2048]{0,1:T(8,128)(2,1)S(1)} %bitcast.199, bf16[128,2048]{0,1:T(8,128)(2,1)S(1)} %copy-done.13, bf16[128,1024]{1,0:T(8,128)(2,1)S(1)} %copy-done.5, f32[1024]{0:T(1024)S(1)} %copy-done.24, ...), kind=kOutput, calls=%fused_computation.108 | convolution fusion | flops 1154252800 | bytes 19345920 | tf_op jit(solution)/shard_map/dot_general | solution.py:212
  246.6 4.2 fusion.33
  250.9 2.1 bitcast_convert_fusion
  252.9 1.7 copy.139
  255.8 71.8 %reduce-scatter.8.cloned.1.call-done = f32[128,1024]{1,0:T(8,128)} async-done(((f32[2048,1024]{1,0:T(8,128)}), f32[128,1024]{1,0:T(8,128)}) %reduce-scatter.8.cloned.1.call-update) | async-done | bytes 524304 | tf_op jit(solution)/shard_map/reduce_scatter | solution.py:176
  327.5 193.4 %reduce-scatter.6.cloned.1.call-done = f32[64,4384]{1,0:T(8,128)} async-done(((f32[1024,4384]{1,0:T(8,128)}), f32[64,4384]{1,0:T(8,128)}) %reduce-scatter.6.cloned.1.call-update) | async-done | bytes 1122320 | tf_op jit(solution)/shard_map/reduce_scatter | solution.py:211
  521.9 6.8 %fusion.51 = (f32[1024]{0:T(1024)S(1)}, f32[128]{0:T(128)S(1)}, f32[128,1024]{1,0:T(8,128)S(1)}) fusion(bf16[128,1024]{1,0:T(8,128)(2,1)S(1)} %copy-done.5, f32[128]{0:T(128)S(1)} %copy-done.62, f32[1024]{0:T(1024)S(1)} %copy-done.24, bf16[1024,4384]{1,0:T(8,128)(2,1)} %all-gather.3.cloned.1.call-done, bf16[128,32]{0,1:T(8,128)(2,1)S(1)} %bitcast.212, ...), kind=kOutput, calls=%fused_computation.90 | convolution fusion | flops 1154644864 | bytes 10896384 | tf_op jit(solution)/shard_map/dot_general | solution.py:207
  528.7 59.6 %all-reduce.16 = (f32[4,2304]{1,0:T(4,128)S(1)}, f32[2304]{0:T(1024)S(1)}, f32[32]{0:T(128)S(1)}, f32[32]{0:T(128)S(1)}, f32[32]{0:T(128)S(1)}, /*index=5*/f32[1024]{0:T(1024)S(1)}, f32[2048]{0:T(1024)S(1)}) all-reduce(f32[4,2304]{1,0:T(4,128)S(1)} %add_dynamic-update-slice_fusion, ...), channel_id=1, replica_groups=mesh['seq'=2,'fsdp'=16] {'fsdp'}, use_global_device_ids=true, to_apply=%region_21.22 | all-reduce | flops 14688 | bytes 117504 | tf_op jit(solution)/shard_map/psum | solution.py:238
  588.3 9.4 %all-reduce.17 = (f32[4,2304]{1,0:T(4,128)}, f32[2304]{0:T(1024)}, f32[32]{0:T(128)}, f32[32]{0:T(128)}, f32[32]{0:T(128)}, /*index=5*/f32[1024]{0:T(1024)}, f32[2048]{0:T(1024)}) all-reduce(f32[4,2304]{1,0:T(4,128)S(1)} %get-tuple-element.320, f32[2304]{0:T(1024)S(1)} %get-tuple-element.321, ...), channel_id=1, replica_groups=mesh['seq'=2,'fsdp'=16] {'seq'}, use_global_device_ids=true, to_apply=%region_22.23 | all-reduce | flops 14688 | bytes 117504 | tf_op jit(solution)/shard_map/psum | solution.py:238
  598.7 2.4 copy.200
  (281 shorter events, 40.1 us)
Async XLA Ops:
  7.2 85.1 %copy-start.4 = (bf16[128,1024]{1,0:T(8,128)(2,1)S(1)}, bf16[128,1024]{1,0:T(8,128)(2,1)}, u32[]{:S(2)}) copy-start(bf16[128,1024]{1,0:T(8,128)(2,1)} %param.16) | copy-start | bytes 786436
  7.2 85.1 %copy-start.23 = (f32[1024]{0:T(1024)S(1)}, f32[1024]{0:T(1024)}, u32[]{:S(2)}) copy-start(f32[1024]{0:T(1024)} %param.25) | copy-start | bytes 12292
  7.2 85.1 %all-gather.3.cloned.1.call-start = ((), (), s32[]{:S(2)}) async-start(), calls=%async_computation.9 | async-start | bytes 9748480 | tf_op jit(solution)/shard_map/all_gather | solution.py:124
  7.9 149.0 %all-gather.5.cloned.1.call-start = ((), (), s32[]{:S(2)}) async-start(), calls=%async_computation.10 | async-start | bytes 4456448 | tf_op jit(solution)/shard_map/all_gather | solution.py:169
  11.6 101.8 %copy-start.78 = (f32[16]{0:T(128)}, f32[16]{0:T(128)S(1)}, u32[]{:S(2)}) copy-start(f32[16]{0:T(128)S(1)} %dynamic_slice.89) | copy-start | bytes 196
  14.3 107.2 %copy-start.31 = (f32[1280]{0:T(1024)}, f32[1280]{0:T(1024)S(1)}, u32[]{:S(2)}) copy-start(f32[1280]{0:T(1024)S(1)} %get-tuple-element.316) | copy-start | bytes 15364
  14.3 107.2 %copy-start.33 = (f32[1280]{0:T(1024)}, f32[1280]{0:T(1024)S(1)}, u32[]{:S(2)}) copy-start(f32[1280]{0:T(1024)S(1)} %get-tuple-element.318) | copy-start | bytes 15364
  14.3 107.2 %copy-start.35 = (f32[1280]{0:T(1024)}, f32[1280]{0:T(1024)S(1)}, u32[]{:S(2)}) copy-start(f32[1280]{0:T(1024)S(1)} %get-tuple-element.319) | copy-start | bytes 15364
  14.3 107.2 %copy-start.37 = (f32[1280]{0:T(1024)}, f32[1280]{0:T(1024)S(1)}, u32[]{:S(2)}) copy-start(f32[1280]{0:T(1024)S(1)} %get-tuple-element.317) | copy-start | bytes 15364
  15.1 98.2 %copy-start.80 = (f32[16]{0:T(128)}, f32[16]{0:T(128)S(1)}, u32[]{:S(2)}) copy-start(f32[16]{0:T(128)S(1)} %fusion.100) | copy-start | bytes 196
  16.0 105.5 %copy-start.76 = (f32[256]{0:T(256)}, f32[256]{0:T(256)S(1)}, u32[]{:S(2)}) copy-start(f32[256]{0:T(256)S(1)} %pad_convert_fusion.1) | copy-start | bytes 3076
  17.8 103.8 %copy-start.70 = (f32[256]{0:T(256)}, f32[256]{0:T(256)S(1)}, u32[]{:S(2)}) copy-start(f32[256]{0:T(256)S(1)} %get-tuple-element.371) | copy-start | bytes 3076
  17.8 103.8 %copy-start.72 = (f32[256]{0:T(256)}, f32[256]{0:T(256)S(1)}, u32[]{:S(2)}) copy-start(f32[256]{0:T(256)S(1)} %get-tuple-element.372) | copy-start | bytes 3076
  20.2 79.4 %copy-start.83 = (f32[128]{0:T(128)}, f32[128]{0:T(128)S(1)}, u32[]{:S(2)}) copy-start(f32[128]{0:T(128)S(1)} %fusion.53) | copy-start | bytes 1540
  20.2 79.4 %copy-start.61 = (f32[128]{0:T(128)}, f32[128]{0:T(128)S(1)}, u32[]{:S(2)}) copy-start(f32[128]{0:T(128)S(1)} %fusion.99) | copy-start | bytes 1540
  99.6 21.7 %copy-start.6 = (bf16[128,4384]{0,1:T(8,128)(2,1)}, bf16[128,4384]{0,1:T(8,128)(2,1)S(1)}, u32[]{:S(2)}) copy-start(bf16[128,4384]{0,1:T(8,128)(2,1)S(1)} %convolution_convert_fusion) | copy-start | bytes 3366916
  100.3 9.2 %all-to-all-start = ((bf16[128,2,16]{0,2,1:T(8,128)(2,1)}), bf16[128,2,16]{0,2,1:T(8,128)(2,1)S(1)}, u32[]{:S(2)}, u32[]{:S(2)}) async-start(bf16[128,2,16]{0,2,1:T(8,128)(2,1)} %bitcast.3), calls=%async_computation | async-start | bytes 16384 | tf_op jit(solution)/shard_map/all_to_all | solution.py:134
  109.5 11.9 %copy-start.39 = (bf16[128,2,16]{0,2,1:T(8,128)(2,1)}, bf16[128,2,16]{0,2,1:T(8,128)(2,1)S(1)}, u32[]{:S(2)}) copy-start(bf16[128,2,16]{0,2,1:T(8,128)(2,1)S(1)} %all-to-all-done) | copy-start | bytes 24580
  109.5 11.6 %all-to-all-start.1 = ((bf16[128,2,1024]{0,2,1:T(8,128)(2,1)}), bf16[128,2,1024]{0,2,1:T(8,128)(2,1)S(1)}, u32[]{:S(2)}, u32[]{:S(2)}) async-start(bf16[128,2,1024]{0,2,1:T(8,128)(2,1)} %bitcast.6), calls=%async_computation.1 | async-start | bytes 1048576 | tf_op jit(solution)/shard_map/all_to_all | solution.py:133
  114.8 6.6 %copy-start.54 = (f32[16,2]{0,1:T(2,128)}, f32[16,2]{0,1:T(2,128)S(1)}, u32[]{:S(2)}) copy-start(f32[16,2]{0,1:T(2,128)S(1)} %slice.164) | copy-start | bytes 388
  114.9 6.5 %copy-start.43 = (f32[16,256]{1,0:T(8,128)}, f32[16,256]{1,0:T(8,128)S(1)}, u32[]{:S(2)}) copy-start(f32[16,256]{1,0:T(8,128)S(1)} %copy_bitcast_fusion) | copy-start | bytes 49156
  129.6 9.6 %copy-start.42 = (f32[256,16]{0,1:T(8,128)}, f32[256,16]{0,1:T(8,128)S(1)}, u32[]{:S(2)}) copy-start(f32[256,16]{0,1:T(8,128)S(1)} %get-tuple-element.362) | copy-start | bytes 49156
  130.9 8.2 %copy-start.25 = (f32[256,256]{1,0:T(8,128)}, f32[256,256]{1,0:T(8,128)S(1)}, u32[]{:S(2)}) copy-start(f32[256,256]{1,0:T(8,128)S(1)} %fusion.73) | copy-start | bytes 786436
  132.9 6.2 %copy-start.16 = (f32[256,1024]{0,1}, f32[256,1024]{0,1:S(1)}, u32[]{:S(2)}) copy-start(f32[256,1024]{0,1:S(1)} %fusion.61) | copy-start | bytes 3145732
  164.0 12.5 %all-to-all-start.3 = ((bf16[128,2,1024]{0,2,1:T(8,128)(2,1)}), bf16[128,2,1024]{0,2,1:T(8,128)(2,1)}, u32[]{:S(2)}, u32[]{:S(2)}) async-start(bf16[128,2,1024]{0,2,1:T(8,128)(2,1)} %bitcast.201), calls=%async_computation.3 | async-start | bytes 1048576 | tf_op jit(solution)/shard_map/all_to_all | solution.py:183
  168.2 61.9 %reduce-scatter.10.cloned.1.call-start = ((), (), s32[]{:S(2)}) async-start(), calls=%async_computation.13 | async-start | bytes 196608
  181.0 5.8 copy-start.18
  181.0 5.8 copy-start.20
  181.0 5.8 copy-start.26
  181.0 5.8 copy-start.28
  198.1 6.2 %copy-start.7 = (f32[256,1280]{1,0:T(8,128)S(1)}, f32[256,1280]{1,0:T(8,128)}, u32[]{:S(2)}) copy-start(f32[256,1280]{1,0:T(8,128)} %get-tuple-element.348) | copy-start | bytes 3932164
  198.1 6.2 %copy-start.11 = (f32[256,1024]{1,0:T(8,128)S(1)}, f32[256,1024]{1,0:T(8,128)}, u32[]{:S(2)}) copy-start(f32[256,1024]{1,0:T(8,128)} %copy.132) | copy-start | bytes 3145732
  198.1 6.2 %copy-start.73 = (f32[256]{0:T(256)S(1)}, f32[256]{0:T(256)}, u32[]{:S(2)}) copy-start(f32[256]{0:T(256)} %copy-done.72) | copy-start | bytes 3076
  209.7 41.1 %copy-start.49 = (f32[1280]{0:T(1024)}, f32[1280]{0:T(1024)S(1)}, u32[]{:S(2)}) copy-start(f32[1280]{0:T(1024)S(1)} %get-tuple-element.312) | copy-start | bytes 15364
  210.4 117.1 %reduce-scatter.8.cloned.1.call-start = ((), (), s32[]{:S(2)}) async-start(), calls=%async_computation.12 | async-start | bytes 8912896 | tf_op jit(solution)/shard_map/reduce_scatter | solution.py:176
  219.5 7.0 %all-to-all-start.5 = ((bf16[2,128,16]{1,2,0:T(8,128)(2,1)}), bf16[2,128,16]{1,2,0:T(8,128)(2,1)S(1)}, u32[]{:S(2)}, u32[]{:S(2)}) async-start(bf16[2,128,16]{1,2,0:T(8,128)(2,1)} %copy_bitcast_fusion.3), calls=%async_computation.5 | async-start | bytes 16384 | tf_op jit(solution)/shard_map/all_to_all | solution.py:197
  222.8 13.8 %copy-start.5 = (bf16[128,1024]{1,0:T(8,128)(2,1)S(1)}, bf16[128,1024]{1,0:T(8,128)(2,1)}, u32[]{:S(2)}) copy-start(bf16[128,1024]{1,0:T(8,128)(2,1)} %param.16) | copy-start | bytes 786436
  222.8 13.8 %copy-start.13 = (bf16[128,2048]{0,1:T(8,128)(2,1)S(1)}, bf16[128,2048]{0,1:T(8,128)(2,1)}, u32[]{:S(2)}) copy-start(bf16[128,2048]{0,1:T(8,128)(2,1)} %get-tuple-element.349) | copy-start | bytes 1572868
  222.8 13.8 %copy-start.24 = (f32[1024]{0:T(1024)S(1)}, f32[1024]{0:T(1024)}, u32[]{:S(2)}) copy-start(f32[1024]{0:T(1024)} %param.25) | copy-start | bytes 12292
  222.9 13.8 %copy-start.62 = (f32[128]{0:T(128)S(1)}, f32[128]{0:T(128)}, u32[]{:S(2)}) copy-start(f32[128]{0:T(128)} %copy-done.61) | copy-start | bytes 1540
  226.6 10.1 %all-to-all-start.4 = ((bf16[2,128,1024]{1,2,0:T(8,128)(2,1)}), bf16[2,128,1024]{1,2,0:T(8,128)(2,1)S(1)}, u32[]{:S(2)}, u32[]{:S(2)}) async-start(bf16[2,128,1024]{1,2,0:T(8,128)(2,1)} %copy.133), calls=%async_computation.4 | async-start | bytes 1048576 | tf_op jit(solution)/shard_map/all_to_all | solution.py:190
  230.1 290.9 %reduce-scatter.6.cloned.1.call-start = ((), (), s32[]{:S(2)}) async-start(), calls=%async_computation.11 | async-start | bytes 19496960 | tf_op jit(solution)/shard_map/reduce_scatter | solution.py:211
  236.6 9.3 %copy-start.14 = (bf16[2,128,1024]{1,2,0:T(8,128)(2,1)}, bf16[2,128,1024]{1,2,0:T(8,128)(2,1)S(1)}, u32[]{:S(2)}) copy-start(bf16[2,128,1024]{1,2,0:T(8,128)(2,1)S(1)} %all-to-all-done.4) | copy-start | bytes 1572868
  246.0 352.7 %all-reduce.21.cloned.1.call-start = ((), (), s32[]{:S(2)}) async-start(), calls=%async_computation.14 | async-start | bytes 3342336 | tf_op jit(solution)/shard_map/psum | solution.py:219
  254.7 266.3 %copy-start.89 = (f32[32]{0:T(128)S(1)}, f32[32]{0:T(128)}, u32[]{:S(2)}) copy-start(f32[32]{0:T(128)} %param.23) | copy-start | bytes 388
  254.8 267.1 %copy-start.15 = (bf16[2,128,1024]{1,2,0:T(8,128)(2,1)S(1)}, bf16[2,128,1024]{1,2,0:T(8,128)(2,1)}, u32[]{:S(2)}) copy-start(bf16[2,128,1024]{1,2,0:T(8,128)(2,1)} %copy-done.14) | copy-start | bytes 1572868
  521.9 6.8 %copy-start.50 = (f32[2048]{0:T(1024)S(1)}, f32[2048]{0:T(1024)}, u32[]{:S(2)}) copy-start(f32[2048]{0:T(1024)} %get-tuple-element.310) | copy-start | bytes 24580
  521.9 75.8 %copy-start.84 = (f32[128]{0:T(128)S(1)}, f32[128]{0:T(128)}, u32[]{:S(2)}) copy-start(f32[128]{0:T(128)} %copy-done.83) | copy-start | bytes 1540
  (53 other events, 133.8 us)
Sparse Core Ops, SparseCore 0:
  10.3 81.9 all-gather.2
  94.5 48.8 all-gather.4
  210.5 9.5 reduce-scatter.9
  224.0 103.4 reduce-scatter.7
  331.6 189.3 reduce-scatter.5
  523.2 52.7 all-reduce.20
